TPU v7x, 32 devices: a whole 2x2x4 slice. The times are simulated.
32 devices in a mesh: range: 4 (over y, core), chan: 8 (over z, x).
Axes of the slice: x: 2, y: 2, z: 4, core: 2. Of those that a mesh axis runs over, the one named last changes fastest.
Arguments:
- echoes: float32 [2, 64, 512, 1024], P(None, 'chan', None, 'range'), may hold values from -18 to 18
- chirp: float32 [2, 129], replicated, may hold values from -0.375 to 0.375
- train_mask: int32 [512, 8], P('chan', 'range'), may hold values from 0 to 1, as said below
Outputs:
- spectra: bfloat16 [2, 512, 64, 1024], P(None, 'chan', None, 'range')
- factors: float32 [512, 2, 128, 128], P('chan')
Inputs may be any that keep to these rules, and one draw needn't show every extreme that they name: `train_mask`: in each Doppler bin exactly 4 consecutive tiles are 0 and all other tiles are 1.
All inputs are finite; a program needn't handle non-finite values.
Results may differ from a plain program's by a relative error of at most 0.001.
Values sent between devices are 32-bit elements; how exact they have to be, the bound alone decides.
A program may use at most 128 MiB of HBM per device.

v0:
```python
import math
import jax
import jax.numpy as jnp
from jax import lax
from jax.sharding import PartitionSpec as P

TILE = 128
best_precision = lax.Precision.HIGHEST


def from_behind(value, axis, steps):
    count = lax.axis_size(axis)
    leading, last = (max(0, -steps), min(count, count - steps))
    return lax.ppermute(value, axis, [(source, source + steps) for source in range(leading, last)])


def from_behind_2(block, axis, distance):
    devices = range(lax.axis_size(axis))
    route = [((i - distance) % len(devices), i) for i in devices]
    return lax.ppermute(block, axis, route)


def toeplitz_rows(taps):
    tap_span = taps.shape[-1] - 1
    padded = jnp.concatenate([taps, jnp.zeros((taps.shape[0], tap_span), taps.dtype)], -1)
    tiled = jnp.tile(padded, (1, tap_span))
    return tiled[:, : 2 * tap_span * tap_span].reshape(taps.shape[0], tap_span, 2 * tap_span)


def compress(extended, taps):
    tap_span = taps.shape[-1] - 1
    lead_shape = extended.shape[:-1]
    block_count = extended.shape[-1] // tap_span - 1
    blocks = extended.reshape(lead_shape + (block_count + 1, tap_span))
    window = jnp.concatenate([blocks[..., :block_count, :], blocks[..., 1:, :]], -1)
    kernel = toeplitz_rows(taps)
    products = jnp.einsum(
        "tcpnk,sok->tscpno",
        window,
        kernel,
        precision=best_precision,
        preferred_element_type=jnp.float32,
    )
    real_part = products[0, 0] + products[1, 1]
    imag_part = products[1, 0] - products[0, 1]
    return jnp.stack([real_part, imag_part]).reshape(lead_shape + (block_count * tap_span,))


def doppler_table(bin_numbers, pulse_count):
    phase_index = (
        bin_numbers[:, None] * jnp.arange(pulse_count, dtype=jnp.int32)[None, :] % pulse_count
    )
    angles = phase_index.astype(jnp.float32) * (2.0 * math.pi / pulse_count)
    scaling = 1.0 / math.sqrt(pulse_count)
    return jnp.stack([jnp.cos(angles) * scaling, -jnp.sin(angles) * scaling])


def doppler(signal, dft_table):
    products = jnp.einsum(
        "sdp,tcpg->stdcg",
        dft_table,
        signal,
        precision=best_precision,
        preferred_element_type=jnp.float32,
    )
    return jnp.stack([products[0, 0] - products[1, 1], products[0, 1] + products[1, 0]])


def gram_block(spectra_now, spectra_next, weights, scaling):
    snapshot = jnp.concatenate([spectra_now, spectra_next], 2)
    masked = snapshot * weights[None, :, None, :]
    products = jnp.einsum(
        "tbkg,sblg->btskl",
        masked,
        snapshot,
        precision=best_precision,
        preferred_element_type=jnp.float32,
    )
    real_part = products[:, 0, 0] + products[:, 1, 1]
    imag_part = products[:, 0, 1] - products[:, 1, 0]
    return jnp.stack([real_part, imag_part], 1) * scaling


def factor(gram):
    order_size = gram.shape[-1]
    strip_size = min(16, order_size)
    columns = jnp.arange(order_size, dtype=jnp.int32)
    remaining = gram
    pieces = []
    for offset in range(0, order_size, strip_size):
        strip_rows = remaining[:, :, :strip_size, :]

        def column_step(position, carry):
            strip_now, found_rows = carry
            place = offset + position
            row_now = lax.dynamic_index_in_dim(strip_now, position, 2, keepdims=False)
            pivots = jnp.sum(jnp.where(columns == place, row_now[:, 0], 0.0), -1)
            inverse = lax.rsqrt(pivots)[:, None]
            row_real = jnp.where(columns >= place, row_now[:, 0] * inverse, 0.0)
            row_imag = jnp.where(columns > place, row_now[:, 1] * inverse, 0.0)
            coef_real = row_real[:, offset : offset + strip_size]
            coef_imag = row_imag[:, offset : offset + strip_size]
            new_real = (
                strip_now[:, 0]
                - coef_real[:, :, None] * row_real[:, None, :]
                - coef_imag[:, :, None] * row_imag[:, None, :]
            )
            new_imag = (
                strip_now[:, 1]
                - coef_real[:, :, None] * row_imag[:, None, :]
                + coef_imag[:, :, None] * row_real[:, None, :]
            )
            found_rows = lax.dynamic_update_index_in_dim(
                found_rows, jnp.stack([row_real, row_imag], 1), position, 2
            )
            return (jnp.stack([new_real, new_imag], 1), found_rows)

        strip_end, found_rows = lax.fori_loop(
            0, strip_size, column_step, (strip_rows, jnp.zeros_like(strip_rows))
        )
        pieces.append(found_rows)
        if offset + strip_size < order_size:
            tail_part = found_rows[:, :, :, offset + strip_size :]
            products = jnp.einsum(
                "nabi,ncbj->nacij",
                tail_part,
                found_rows,
                precision=best_precision,
                preferred_element_type=jnp.float32,
            )
            update_real = products[:, 0, 0] + products[:, 1, 1]
            update_imag = products[:, 0, 1] - products[:, 1, 0]
            remaining = remaining[:, :, strip_size:, :] - jnp.stack([update_real, update_imag], 1)
    return jnp.concatenate(pieces, 2)


def on_device(echoes, chirp, train_mask):
    tap_span = chirp.shape[-1] - 1
    pulses = echoes.shape[2]
    gate_count = echoes.shape[3]
    rim_gates = from_behind(echoes[..., :tap_span], "range", -1)
    compressed = compress(jnp.concatenate([echoes, rim_gates], -1), chirp)
    spectra_all = doppler(compressed, doppler_table(jnp.arange(pulses, dtype=jnp.int32), pulses))
    turned = lax.all_to_all(spectra_all, "chan", split_axis=1, concat_axis=2, tiled=True)
    edge_bin = from_behind_2(turned[:, :1], "chan", -1)
    following = jnp.concatenate([turned[:, 1:], edge_bin], 1)
    spectra_out = turned.astype(jnp.bfloat16)
    total_gates = gate_count * lax.axis_size("range")
    scaling = 1.0 / total_gates
    weights = jnp.broadcast_to(
        train_mask.astype(jnp.float32)[:, :, None], train_mask.shape + (TILE,)
    ).reshape(train_mask.shape[0], gate_count)
    partial_gram = lax.psum_scatter(
        gram_block(turned, following, weights, scaling), "range", scatter_dimension=0, tiled=True
    )
    factors = lax.all_gather(factor(partial_gram), "range", axis=0, tiled=True)
    return (spectra_out, factors)


def solution(mesh):
    return jax.shard_map(
        on_device,
        mesh=mesh,
        in_specs=(P(None, "chan", None, "range"), P(), P("chan", "range")),
        out_specs=(P(None, "chan", None, "range"), P("chan", None, None, None)),
        check_vma=False,
    )
```

profile of v0, /device:TPU:0, one launch (start us, length us, event | category | flops | bytes accessed | tf_op | source)
XLA Modules:
  0.0 662.5 jit_solution(18391180482651036311)
XLA Ops:
  7.2 8.7 %copy.189 = f32[2,8,512,256]{2,3,1,0:T(8,128)} copy(f32[2,8,512,256]{3,2,1,0:T(8,128)} %param.19) | data formatting | bytes 16777216 | tf_op args[0]
  15.9 4.8 slice.757
  20.7 1.3 collective-permute-start
  22.6 4.2 negate_multiply_fusion
  26.7 3.4 collective-permute-done
  30.1 6.2 pad_maximum_fusion.8
  36.3 7.0 %fusion.104 = (f32[2,8,512,2,128]{2,4,3,1,0:T(8,128)}, f32[2,8,512,2,128]{2,4,3,1,0:T(8,128)}) fusion(f32[2,8,512,3,128]{2,4,3,1,0:T(8,128)S(1)} %bitcast.399), kind=kLoop, calls=%fused_computation.288 | loop fusion | bytes 33554432 | tf_op jit(solution)/shard_map/slice | solution.py:35
  43.3 8.7 %copy.286 = f32[2,8,512,2,128]{4,2,3,1,0:T(8,128)} copy(f32[2,8,512,2,128]{2,4,3,1,0:T(8,128)} %get-tuple-element.1093) | data formatting | bytes 16777216
  52.0 8.7 %copy.285 = f32[2,8,512,2,128]{4,2,3,1,0:T(8,128)} copy(f32[2,8,512,2,128]{2,4,3,1,0:T(8,128)} %get-tuple-element.1092) | data formatting | bytes 16777216
  60.7 21.7 %fusion.55 = f32[2,2,8,512,2,128]{3,5,4,2,0,1:T(8,128)} fusion(f32[2,8,512,2,128]{4,2,3,1,0:T(8,128)} %copy.286, f32[2,8,512,2,128]{4,2,3,1,0:T(8,128)} %copy.285, f32[1,2,128,256]{3,1,2,0:T(2,128)S(1)} %bitcast.450), kind=kOutput, calls=%fused_computation.179 | convolution fusion | flops 12889096192 | bytes 33816576 | tf_op jit(solution)/shard_map/tcpnk,sok->tscpno/dot_general | solution.py:37
  82.5 10.2 %slice_add_fusion.1 = (f32[1,1,8,512,2,128]{3,5,4,2,0,1:T(8,128)S(1)}, f32[1,1,8,512,2,128]{3,5,4,2,0,1:T(8,128)}) fusion(f32[2,2,8,512,2,128]{3,5,4,2,0,1:T(8,128)} %fusion.55), kind=kLoop, calls=%fused_computation.194 | loop fusion | flops 2097152 | bytes 25165824 | tf_op jit(solution)/shard_map/add | solution.py:44
  92.6 31.7 %fusion.56 = f32[2,2,512,8,256]{2,4,0,3,1:T(8,128)S(1)} fusion(f32[1,8,512,256]{2,3,1,0:T(8,128)} %bitcast.409, f32[1,8,512,256]{2,3,1,0:T(8,128)S(1)} %bitcast.408, f32[1,512,512]{2,1,0:T(8,128)S(1)} %get-tuple-element.1118, f32[1,512,512]{2,1,0:T(8,128)S(1)} %get-tuple-element.1119), kind=kOutput, calls=%fused_computation.180 | convolution fusion | flops 25772425216 | bytes 27262976 | tf_op jit(solution)/shard_map/sdp,tcpg->stdcg/dot_general | solution.py:59
  126.4 4.4 pad_maximum_fusion.9
  130.7 10.3 %copy.194 = f32[2,512,8,256]{3,2,0,1:T(8,128)} copy(f32[2,512,8,256]{1,3,2,0:T(8,128)} %pad_maximum_fusion.9) | data formatting | bytes 16777216 | tf_op jit(solution)/shard_map/stack | solution.py:66
  141.1 177.9 %all_to_all.18 = f32[2,512,8,256]{3,2,0,1:T(8,128)S(1)} all-to-all(f32[2,512,8,256]{3,2,0,1:T(8,128)} %copy.194), channel_id=1, replica_groups=mesh['range'=4,'chan'=8] {'chan'}, dimensions={1} | all-to-all | bytes 16777216 | tf_op jit(solution)/shard_map/all_to_all | solution.py:144
  319.0 1.3 copy.366
  320.3 2.2 copy-done
  322.5 3.3 copy-done.1
  325.8 3.1 collective-permute-start.1
  329.2 7.6 %slice.768 = f32[2,63,64,256]{3,2,0,1:T(8,128)} slice(f32[2,64,64,256]{3,2,0,1:T(8,128)} %bitcast.402), slice={[0:2], [1:64], [0:64], [0:256]} | slice | bytes 16515072 | tf_op jit(solution)/shard_map/slice | solution.py:146
  336.8 27.5 %fusion.46 = f32[64,2,2,128,128]{3,4,1,2,0:T(8,128)} fusion(f32[2,1,64,256]{3,2,0,1:T(8,128)S(1)} %collective-permute-done.1, f32[2,63,64,256]{3,2,0,1:T(8,128)} %slice.768, f32[2,64,64,256]{3,2,0,1:T(8,128)} %bitcast.403, f32[64,256]{1,0:T(8,128)S(1)} %bitcast.452), kind=kOutput, calls=%fused_computation.169 | convolution fusion | flops 12905873408 | bytes 33619968 | tf_op jit(solution)/shard_map/tbkg,sblg->btskl/dot_general | solution.py:72
  364.3 4.2 fusion.57
  368.5 4.2 fusion.59
  372.8 1.6 maximum_multiply_fusion
  375.5 8.0 %copy.365 = f32[8,8,256,128]{3,1,2,0:T(8,128)} copy(f32[8,8,256,128]{3,2,1,0:T(8,128)S(1)} %bitcast.404) | data formatting | bytes 16777216
  383.6 82.1 %reduce-scatter.5.cloned.1.call-done = f32[16,32768]{1,0:T(8,128)} async-done(((f32[64,32768]{1,0:T(8,128)}), f32[16,32768]{1,0:T(8,128)}) %reduce-scatter.5.cloned.1.call-update) | async-done | bytes 2097168
  465.7 2.0 copy.300
  467.7 1.9 slice.775
  470.2 8.8 %while.136 = (s32[]{:T(128)}, f32[16,2,16,128]{3,2,1,0:T(8,128)S(1)}, f32[16,2,16,128]{3,0,1,2:T(8,128)S(1)}, s32[]{:T(128)}) while((s32[]{:T(128)}, f32[16,2,16,128]{3,2,1,0:T(8,128)S(1)}, f32[16,2,16,128]{3,0,1,2:T(8,128)S(1)}, s32[]{:T(128)}) %tuple.404), condition=%wide.region_3.4_spmd.clone.clone, body=%wide.region_1.3_spmd.clone.clone.sunk | while | flops 345458 | bytes 1227949 | solution.py:118
  479.9 3.3 convolution_bitcast_fusion
  484.3 1.7 copy.292
  486.1 1.9 maximum_subtract_fusion
  488.1 11.2 %while.137 = (s32[]{:T(128)}, f32[16,2,16,128]{3,2,1,0:T(8,128)S(1)}, f32[16,2,16,128]{3,0,1,2:T(8,128)S(1)}, s32[]{:T(128)}, s32[]{:T(128)}) while((s32[]{:T(128)}, f32[16,2,16,128]{3,2,1,0:T(8,128)S(1)}, f32[16,2,16,128]{3,0,1,2:T(8,128)S(1)}, s32[]{:T(128)}, s32[]{:T(128)}) %tuple.407), condition=%wide.region_6.7_spmd.clone.clone, body=%wide.region_4.6_spmd.clone.clone.sunk | while | flops 345459 | bytes 1228033 | solution.py:118
  500.1 2.9 convolution_bitcast_fusion.1
  504.7 11.2 %while.138 = (s32[]{:T(128)}, f32[16,2,16,128]{3,2,1,0:T(8,128)S(1)}, f32[16,2,16,128]{3,0,1,2:T(8,128)S(1)}, s32[]{:T(128)}, s32[]{:T(128)}) while((s32[]{:T(128)}, f32[16,2,16,128]{3,2,1,0:T(8,128)S(1)}, f32[16,2,16,128]{3,0,1,2:T(8,128)S(1)}, s32[]{:T(128)}, s32[]{:T(128)}) %tuple.410), condition=%wide.region_9.10_spmd.clone.clone, body=%wide.region_7.9_spmd.clone.clone.sunk | while | flops 345459 | bytes 1228033 | solution.py:118
  516.8 2.4 convolution_bitcast_fusion.2
  519.6 11.4 %while.139 = (s32[]{:T(128)}, f32[16,2,16,128]{3,2,1,0:T(8,128)S(1)}, f32[16,2,16,128]{3,0,1,2:T(8,128)S(1)}, s32[]{:T(128)}, s32[]{:T(128)}) while((s32[]{:T(128)}, f32[16,2,16,128]{3,2,1,0:T(8,128)S(1)}, f32[16,2,16,128]{3,0,1,2:T(8,128)S(1)}, s32[]{:T(128)}, s32[]{:T(128)}) %tuple.413), condition=%wide.region_12.13_spmd.clone.clone, body=%wide.region_10.12_spmd.clone.clone.sunk | while | flops 345459 | bytes 1228033 | solution.py:118
  531.9 2.0 convolution_bitcast_fusion.3
  534.4 11.2 %while.140 = (s32[]{:T(128)}, f32[16,2,16,128]{3,2,1,0:T(8,128)S(1)}, f32[16,2,16,128]{3,0,1,2:T(8,128)S(1)}, s32[]{:T(128)}, s32[]{:T(128)}) while((s32[]{:T(128)}, f32[16,2,16,128]{3,2,1,0:T(8,128)S(1)}, f32[16,2,16,128]{3,0,1,2:T(8,128)S(1)}, s32[]{:T(128)}, s32[]{:T(128)}) %tuple.416), condition=%wide.region_15.16_spmd.clone.clone, body=%wide.region_13.15_spmd.clone.clone.sunk | while | flops 345459 | bytes 1228033 | solution.py:118
  546.4 1.6 convolution_bitcast_fusion.4
  548.3 11.2 %while.141 = (s32[]{:T(128)}, f32[16,2,16,128]{3,2,1,0:T(8,128)S(1)}, f32[16,2,16,128]{3,0,1,2:T(8,128)S(1)}, s32[]{:T(128)}, s32[]{:T(128)}) while((s32[]{:T(128)}, f32[16,2,16,128]{3,2,1,0:T(8,128)S(1)}, f32[16,2,16,128]{3,0,1,2:T(8,128)S(1)}, s32[]{:T(128)}, s32[]{:T(128)}) %tuple.419), condition=%wide.region_18.19_spmd.clone.clone, body=%wide.region_16.18_spmd.clone.clone.sunk | while | flops 345459 | bytes 1228033 | solution.py:118
  560.4 1.3 convolution_bitcast_fusion.5
  561.9 11.2 %while.142 = (s32[]{:T(128)}, f32[16,2,16,128]{3,2,1,0:T(8,128)S(1)}, f32[16,2,16,128]{3,0,1,2:T(8,128)S(1)}, s32[]{:T(128)}, s32[]{:T(128)}) while((s32[]{:T(128)}, f32[16,2,16,128]{3,2,1,0:T(8,128)S(1)}, f32[16,2,16,128]{3,0,1,2:T(8,128)S(1)}, s32[]{:T(128)}, s32[]{:T(128)}) %tuple.422), condition=%wide.region_21.22_spmd.clone.clone, body=%wide.region_19.21_spmd.clone.clone.sunk | while | flops 345459 | bytes 1228033 | solution.py:118
  575.4 13.0 %while.143 = (s32[]{:T(128)}, f32[16,2,16,128]{3,2,1,0:T(8,128)S(1)}, f32[16,2,16,128]{3,2,1,0:T(8,128)S(1)}, s32[]{:T(128)}, s32[]{:T(128)}, /*index=5*/s32[]{:T(128)}) while((s32[]{:T(128)}, f32[16,2,16,128]{3,2,1,0:T(8,128)S(1)}, f32[16,2,16,128]{3,2,1,0:T(8,128)S(1)}, s32[]{:T(128)}, s32[]{:T(128)}, ...), condition=%wide.region_24.25_spmd.clone.clone, body=%wide.region_22.24_spmd.clone.clone.sunk | while | flops 345459 | bytes 1293577 | solution.py:118
  589.2 4.0 copy.368
  593.2 2.3 copy.239
  595.5 52.1 %all-gather.2.cloned.1.call-done = f32[64,2,128,128]{3,2,1,0:T(8,128)} async-done(((f32[16,2,128,128]{3,2,1,0:T(8,128)}), f32[64,2,128,128]{3,2,1,0:T(8,128)}) %all-gather.2.cloned.1.call-update) | async-done | bytes 8388624 | tf_op jit(solution)/shard_map/all_gather | solution.py:156
  647.6 7.9 %copy.476 = f32[64,2,128,128]{3,2,1,0:T(8,128)} copy(f32[64,2,128,128]{3,2,1,0:T(8,128)} %all-gather.2.cloned.1.call-done) | data formatting | bytes 16777216
  (1742 shorter events, 96.3 us)
Async XLA Ops:
  7.2 458.5 %reduce-scatter.5.cloned.1.call-start = ((), (), s32[]{:S(2)}) async-start(), calls=%async_computation.3 | async-start | bytes 10485760
  15.9 6.1 copy-start.6
  20.7 9.4 %collective-permute-start = (f32[2,8,512,128]{2,3,1,0:T(8,128)}, f32[2,8,512,128]{2,3,1,0:T(8,128)}, u32[]{:S(2)}, u32[]{:S(2)}) collective-permute-start(f32[2,8,512,128]{2,3,1,0:T(8,128)} %slice.757), channel_id=1, source_target_pairs={{8,0},{16,8},{24,16},{9,1},{17,9},{25,17},{10,2},{18,10},{26,18},{... | collective-permute-start | bytes 12582920 | tf_op jit(solution)/shard_map/ppermute | solution.py:14
  22.6 13.7 %copy-start.5 = (f32[2,32896]{1,0:T(2,128)}, f32[2,32896]{1,0:T(2,128)S(1)}, u32[]{:S(2)}) copy-start(f32[2,32896]{1,0:T(2,128)S(1)} %tile.10) | copy-start | bytes 789508
  52.0 8.7 %slice-start = ((f32[2,32896]{1,0:T(2,128)}), f32[2,32768]{1,0:T(2,128)S(1)}, s32[]{:S(2)}) async-start(f32[2,32896]{1,0:T(2,128)} %copy-done.5), calls=%async_computation.4 | async-start | bytes 524288 | tf_op jit(solution)/shard_map/slice | solution.py:27
  319.0 3.5 copy-start
  319.0 9.9 %copy-start.7 = (s32[64,2]{0,1:T(2,128)S(1)}, s32[64,2]{0,1:T(2,128)}, u32[]{:S(2)}) copy-start(s32[64,2]{0,1:T(2,128)} %param.21) | copy-start | bytes 1540
  322.5 3.3 copy-start.1
  325.8 11.0 %collective-permute-start.1 = (f32[2,1,64,256]{3,2,0,1:T(8,128)S(1)}, f32[2,1,64,256]{3,2,0,1:T(8,128)S(1)}, u32[]{:S(2)}, u32[]{:S(2)}) collective-permute-start(f32[2,1,64,256]{3,2,0,1:T(8,128)S(1)} %slice.769), channel_id=1, source_target_pairs={{1,0},{2,1},{3,2},{4,3},{5,4},{6,5},{7,6},{0,7},{9,8},{10,9},{11,1... | collective-permute-start | bytes 393224 | tf_op jit(solution)/shard_map/ppermute | solution.py:20
  383.6 264.0 %all-gather.2.cloned.1.call-start = ((), (), s32[]{:S(2)}) async-start(), calls=%async_computation.2 | async-start | bytes 10485760 | tf_op jit(solution)/shard_map/all_gather | solution.py:156
  479.9 4.4 copy-start.2
  503.5 1.1 copy-start.3
  515.9 3.5 copy-start.4
Sparse Core Ops, SparseCore 0:
  383.7 81.9 reduce-scatter.4
  589.3 58.2 all-gather.1
where the time goes:
time: 668 us; the launch traced here: 663 us
  blocking collectives  178 us (27%)
  waiting for transfers between devices  138 us (21%)
  local copies, waits for them, and re-layouts  124 us (19%)
  other arithmetic  98.7 us (15%)
  matrix products  95.1 us (14%)
  between operations  14.8 us (2%)
  loops' own time  9.7 us (1%)
    all_to_all x1, blocking collectives, on_device(): lax.all_to_all(spectra_all, 'chan', split_axis=1, concat_axis=2, tiled=True)  178 us
    unnamed x3, waiting for transfers between devices  82.1 us
    unnamed x35, local copies, waits for them, and re-layouts  57.4 us
    all_gather x1, waiting for transfers between devices, on_device(): factors = lax.all_gather(factor(partial_gram), 'range', axis=0, tiled=True)  52.1 us
    dot_general x1, matrix products, doppler(): jnp.einsum('sdp,tcpg->stdcg', dft_table, signal, precision=best_precision...  31.7 us
    dot_general x1, matrix products, gram_block(): jnp.einsum('tbkg,sblg->btskl', masked, snapshot, precision=best_precision...  27.5 us
    dot_general x1, matrix products, compress(): jnp.einsum('tcpnk,sok->tscpno', window, kernel, precision=best_precision,...  21.7 us
    select_n x256, other arithmetic, column_step(): row_real = jnp.where(columns >= place, row_now[:, 0] * inverse, 0.0)  19 us
  transfers between devices with their start and end apart: 4, of which 3 were waited for; matrix products, arithmetic and copies ran while one was open for 3% of the time, Pallas kernels for 0%

commit v1 on v0

--- a/solution.py
+++ b/solution.py
@@ -153,7 +153,10 @@
     partial_gram = lax.psum_scatter(
         gram_block(turned, following, weights, scaling), "range", scatter_dimension=0, tiled=True
     )
-    factors = lax.all_gather(factor(partial_gram), "range", axis=0, tiled=True)
+    factors = jnp.concatenate(
+        lax.all_to_all(jnp.stack([factor(partial_gram)] * lax.axis_size("range")), "range", 0, 0),
+        axis=0,
+    )
     return (spectra_out, factors)
 
 

time: 668 us -> 713 us (1.067)
  waiting for transfers between devices: 138 us -> 172 us
    all_to_all x0 -> x1, waiting for transfers between devices: none -> 86.8 us  [on_device(): lax.all_to_all(jnp.stack([factor(partial_gram)] * lax.axis_size('range'))...]
    all_gather x1 -> x0, waiting for transfers between devices: 52.1 us -> none  [on_device(): factors = lax.all_gather(factor(partial_gram), 'range', axis=0, tiled=True)]
    unnamed x35 -> x47, local copies, waits for them, and re-layouts: 57.4 us -> 61.1 us
    unnamed x3 -> x2, waiting for transfers between devices: 82.1 us -> 82.2 us
where the time goes in v1:
time: 713 us; the launch traced here: 708 us
  blocking collectives  178 us (25%)
  waiting for transfers between devices  172 us (24%)
  local copies, waits for them, and re-layouts  128 us (18%)
  other arithmetic  98.8 us (14%)
  matrix products  96.1 us (13%)
  between operations  14.9 us (2%)
  starting transfers between devices  10.1 us (1%)
  loops' own time  9.45 us (1%)
    all_to_all x1, blocking collectives, on_device(): lax.all_to_all(spectra_all, 'chan', split_axis=1, concat_axis=2, tiled=True)  178 us
    all_to_all x1, waiting for transfers between devices, on_device(): lax.all_to_all(jnp.stack([factor(partial_gram)] * lax.axis_size('range'))...  86.8 us
    unnamed x2, waiting for transfers between devices  82.2 us
    unnamed x47, local copies, waits for them, and re-layouts  61.1 us
    dot_general x1, matrix products, doppler(): jnp.einsum('sdp,tcpg->stdcg', dft_table, signal, precision=best_precision...  31.7 us
    dot_general x1, matrix products, gram_block(): jnp.einsum('tbkg,sblg->btskl', masked, snapshot, precision=best_precision...  27.5 us
    dot_general x1, matrix products, compress(): jnp.einsum('tcpnk,sok->tscpno', window, kernel, precision=best_precision,...  21.7 us
    select_n x256, other arithmetic, column_step(): row_real = jnp.where(columns >= place, row_now[:, 0] * inverse, 0.0)  19 us
  transfers between devices with their start and end apart: 4, of which 3 were waited for; matrix products, arithmetic and copies ran while one was open for 3% of the time, Pallas kernels for 0%

profile of v1, /device:TPU:0, one launch (start us, length us, event | category | flops | bytes accessed | tf_op | source)
XLA Modules:
  0.0 707.7 jit_solution(6341201973405232020)
XLA Ops:
  7.2 8.7 %copy.168 = f32[2,8,512,256]{2,3,1,0:T(8,128)} copy(f32[2,8,512,256]{3,2,1,0:T(8,128)} %param.19) | data formatting | bytes 16777216 | tf_op args[0]
  15.9 4.8 slice.757
  22.6 4.2 negate_multiply_fusion
  26.7 3.4 collective-permute-done
  30.1 6.2 pad_maximum_fusion.8
  36.3 7.0 fusion.105
  43.3 8.8 %copy.256 = f32[2,8,512,2,128]{4,2,3,1,0:T(8,128)} copy(f32[2,8,512,2,128]{2,4,3,1,0:T(8,128)} %get-tuple-element.1093) | data formatting | bytes 16777216
  52.1 8.8 %copy.255 = f32[2,8,512,2,128]{4,2,3,1,0:T(8,128)} copy(f32[2,8,512,2,128]{2,4,3,1,0:T(8,128)} %get-tuple-element.1092) | data formatting | bytes 16777216
  60.8 21.7 %fusion.56 = f32[2,2,8,512,2,128]{3,5,4,2,0,1:T(8,128)} fusion(f32[2,8,512,2,128]{4,2,3,1,0:T(8,128)} %copy.256, f32[2,8,512,2,128]{4,2,3,1,0:T(8,128)} %copy.255, f32[1,2,128,256]{3,1,2,0:T(2,128)S(1)} %bitcast.453), kind=kOutput, calls=%fused_computation.180 | convolution fusion | flops 12889096192 | bytes 33816576 | tf_op jit(solution)/shard_map/tcpnk,sok->tscpno/dot_general | solution.py:37
  82.6 10.2 %slice_add_fusion.1 = (f32[1,1,8,512,2,128]{3,5,4,2,0,1:T(8,128)S(1)}, f32[1,1,8,512,2,128]{3,5,4,2,0,1:T(8,128)}) fusion(f32[2,2,8,512,2,128]{3,5,4,2,0,1:T(8,128)} %fusion.56), kind=kLoop, calls=%fused_computation.195 | loop fusion | flops 2097152 | bytes 25165824 | tf_op jit(solution)/shard_map/add | solution.py:44
  92.8 31.7 %fusion.57 = f32[2,2,512,8,256]{2,4,0,3,1:T(8,128)S(1)} fusion(f32[1,8,512,256]{2,3,1,0:T(8,128)} %bitcast.412, f32[1,8,512,256]{2,3,1,0:T(8,128)S(1)} %bitcast.411, f32[1,512,512]{2,1,0:T(8,128)S(1)} %get-tuple-element.1106, f32[1,512,512]{2,1,0:T(8,128)S(1)} %get-tuple-element.1107), kind=kOutput, calls=%fused_computation.181 | convolution fusion | flops 25772425216 | bytes 27262976 | tf_op jit(solution)/shard_map/sdp,tcpg->stdcg/dot_general | solution.py:59
  126.5 4.4 pad_maximum_fusion.9
  130.8 10.3 %copy.173 = f32[2,512,8,256]{3,2,0,1:T(8,128)} copy(f32[2,512,8,256]{1,3,2,0:T(8,128)} %pad_maximum_fusion.9) | data formatting | bytes 16777216 | tf_op jit(solution)/shard_map/stack | solution.py:66
  141.2 177.9 %all_to_all.23 = f32[2,512,8,256]{3,2,0,1:T(8,128)S(1)} all-to-all(f32[2,512,8,256]{3,2,0,1:T(8,128)} %copy.173), channel_id=1, replica_groups=mesh['range'=4,'chan'=8] {'chan'}, dimensions={1} | all-to-all | bytes 16777216 | tf_op jit(solution)/shard_map/all_to_all | solution.py:144
  320.4 2.2 copy-done
  322.6 3.3 copy-done.1
  325.9 3.1 collective-permute-start.1
  329.3 7.6 %slice.768 = f32[2,63,64,256]{3,2,0,1:T(8,128)} slice(f32[2,64,64,256]{3,2,0,1:T(8,128)} %bitcast.404), slice={[0:2], [1:64], [0:64], [0:256]} | slice | bytes 16515072 | tf_op jit(solution)/shard_map/slice | solution.py:146
  336.9 27.5 %fusion.47 = f32[64,2,2,128,128]{3,4,1,2,0:T(8,128)} fusion(f32[2,1,64,256]{3,2,0,1:T(8,128)S(1)} %collective-permute-done.1, f32[2,63,64,256]{3,2,0,1:T(8,128)} %slice.768, f32[2,64,64,256]{3,2,0,1:T(8,128)} %bitcast.405, f32[64,256]{1,0:T(8,128)S(1)} %bitcast.455), kind=kOutput, calls=%fused_computation.170 | convolution fusion | flops 12905873408 | bytes 33619968 | tf_op jit(solution)/shard_map/tbkg,sblg->btskl/dot_general | solution.py:72
  364.4 4.2 fusion.58
  368.6 4.2 fusion.60
  372.9 1.6 maximum_multiply_fusion
  375.6 8.0 %copy.321 = f32[8,8,256,128]{3,1,2,0:T(8,128)} copy(f32[8,8,256,128]{3,2,1,0:T(8,128)S(1)} %bitcast.407) | data formatting | bytes 16777216
  383.7 82.1 %reduce-scatter.5.cloned.1.call-done = f32[16,32768]{1,0:T(8,128)} async-done(((f32[64,32768]{1,0:T(8,128)}), f32[16,32768]{1,0:T(8,128)}) %reduce-scatter.5.cloned.1.call-update) | async-done | bytes 2097168
  465.8 2.0 copy.269
  467.8 2.0 slice.775
  470.4 8.8 %while.136 = (s32[]{:T(128)}, f32[16,2,16,128]{3,2,1,0:T(8,128)S(1)}, f32[16,2,16,128]{3,0,1,2:T(8,128)S(1)}, s32[]{:T(128)}) while((s32[]{:T(128)}, f32[16,2,16,128]{3,2,1,0:T(8,128)S(1)}, f32[16,2,16,128]{3,0,1,2:T(8,128)S(1)}, s32[]{:T(128)}) %tuple.398), condition=%wide.region_3.4_spmd.clone.clone, body=%wide.region_1.3_spmd.clone.clone.sunk | while | flops 345458 | bytes 1227949 | solution.py:118
  480.1 3.3 convolution_bitcast_fusion
  484.5 1.7 copy.262
  486.3 1.9 maximum_subtract_fusion
  488.3 11.2 %while.137 = (s32[]{:T(128)}, f32[16,2,16,128]{3,2,1,0:T(8,128)S(1)}, f32[16,2,16,128]{3,0,1,2:T(8,128)S(1)}, s32[]{:T(128)}, s32[]{:T(128)}) while((s32[]{:T(128)}, f32[16,2,16,128]{3,2,1,0:T(8,128)S(1)}, f32[16,2,16,128]{3,0,1,2:T(8,128)S(1)}, s32[]{:T(128)}, s32[]{:T(128)}) %tuple.401), condition=%wide.region_6.7_spmd.clone.clone, body=%wide.region_4.6_spmd.clone.clone.sunk | while | flops 345459 | bytes 1228033 | solution.py:118
  500.3 2.9 convolution_bitcast_fusion.1
  504.9 11.2 %while.138 = (s32[]{:T(128)}, f32[16,2,16,128]{3,2,1,0:T(8,128)S(1)}, f32[16,2,16,128]{3,0,1,2:T(8,128)S(1)}, s32[]{:T(128)}, s32[]{:T(128)}) while((s32[]{:T(128)}, f32[16,2,16,128]{3,2,1,0:T(8,128)S(1)}, f32[16,2,16,128]{3,0,1,2:T(8,128)S(1)}, s32[]{:T(128)}, s32[]{:T(128)}) %tuple.404), condition=%wide.region_9.10_spmd.clone.clone, body=%wide.region_7.9_spmd.clone.clone.sunk | while | flops 345459 | bytes 1228033 | solution.py:118
  517.0 2.4 convolution_bitcast_fusion.2
  519.8 11.4 %while.139 = (s32[]{:T(128)}, f32[16,2,16,128]{3,2,1,0:T(8,128)S(1)}, f32[16,2,16,128]{3,0,1,2:T(8,128)S(1)}, s32[]{:T(128)}, s32[]{:T(128)}) while((s32[]{:T(128)}, f32[16,2,16,128]{3,2,1,0:T(8,128)S(1)}, f32[16,2,16,128]{3,0,1,2:T(8,128)S(1)}, s32[]{:T(128)}, s32[]{:T(128)}) %tuple.407), condition=%wide.region_12.13_spmd.clone.clone, body=%wide.region_10.12_spmd.clone.clone.sunk | while | flops 345459 | bytes 1228033 | solution.py:118
  532.1 2.0 convolution_bitcast_fusion.3
  534.6 11.2 %while.140 = (s32[]{:T(128)}, f32[16,2,16,128]{3,2,1,0:T(8,128)S(1)}, f32[16,2,16,128]{3,0,1,2:T(8,128)S(1)}, s32[]{:T(128)}, s32[]{:T(128)}) while((s32[]{:T(128)}, f32[16,2,16,128]{3,2,1,0:T(8,128)S(1)}, f32[16,2,16,128]{3,0,1,2:T(8,128)S(1)}, s32[]{:T(128)}, s32[]{:T(128)}) %tuple.410), condition=%wide.region_15.16_spmd.clone.clone, body=%wide.region_13.15_spmd.clone.clone.sunk | while | flops 345459 | bytes 1228033 | solution.py:118
  548.5 11.2 %while.141 = (s32[]{:T(128)}, f32[16,2,16,128]{3,2,1,0:T(8,128)S(1)}, f32[16,2,16,128]{3,0,1,2:T(8,128)S(1)}, s32[]{:T(128)}, s32[]{:T(128)}) while((s32[]{:T(128)}, f32[16,2,16,128]{3,2,1,0:T(8,128)S(1)}, f32[16,2,16,128]{3,0,1,2:T(8,128)S(1)}, s32[]{:T(128)}, s32[]{:T(128)}) %tuple.413), condition=%wide.region_18.19_spmd.clone.clone, body=%wide.region_16.18_spmd.clone.clone.sunk | while | flops 345459 | bytes 1228033 | solution.py:118
  562.2 11.2 %while.142 = (s32[]{:T(128)}, f32[16,2,16,128]{3,2,1,0:T(8,128)S(1)}, f32[16,2,16,128]{3,0,1,2:T(8,128)S(1)}, s32[]{:T(128)}, s32[]{:T(128)}) while((s32[]{:T(128)}, f32[16,2,16,128]{3,2,1,0:T(8,128)S(1)}, f32[16,2,16,128]{3,0,1,2:T(8,128)S(1)}, s32[]{:T(128)}, s32[]{:T(128)}) %tuple.416), condition=%wide.region_21.22_spmd.clone.clone, body=%wide.region_19.21_spmd.clone.clone.sunk | while | flops 345459 | bytes 1228033 | solution.py:118
  573.4 2.0 copy.206
  575.4 1.7 convolution_bitcast_fusion.6
  577.2 11.2 %while.143 = (s32[]{:T(128)}, f32[16,2,16,128]{3,2,1,0:T(8,128)S(1)}, f32[16,2,16,128]{3,0,1,2:T(8,128)S(1)}, s32[]{:T(128)}, s32[]{:T(128)}) while((s32[]{:T(128)}, f32[16,2,16,128]{3,2,1,0:T(8,128)S(1)}, f32[16,2,16,128]{3,0,1,2:T(8,128)S(1)}, s32[]{:T(128)}, s32[]{:T(128)}) %tuple.419), condition=%wide.region_24.25_spmd.clone.clone, body=%wide.region_22.24_spmd.clone.clone.sunk | while | flops 345459 | bytes 1228033 | solution.py:118
  589.6 4.3 stack.249
  593.9 5.7 all-to-all-start.1
  599.6 4.0 copy.324
  603.6 2.3 copy.211
  605.9 86.8 %all-to-all-done.1 = f32[4,16,2,128,128]{4,3,2,1,0:T(8,128)} async-done(((f32[4,16,2,128,128]{4,3,2,1,0:T(8,128)}), f32[4,16,2,128,128]{4,3,2,1,0:T(8,128)}, u32[]{:S(2)}, u32[]{:S(2)}) %all-to-all-start.1) | async-done | bytes 8388640 | tf_op jit(solution)/shard_map/all_to_all | solution.py:157
  692.7 7.9 %copy.432 = f32[64,2,128,128]{3,2,1,0:T(8,128)} copy(f32[64,2,128,128]{3,2,1,0:T(8,128)} %bitcast.60) | data formatting | bytes 16777216
  (1723 shorter events, 98.5 us)
Async XLA Ops:
  7.2 458.7 %reduce-scatter.5.cloned.1.call-start = ((), (), s32[]{:S(2)}) async-start(), calls=%async_computation.3 | async-start | bytes 10485760
  15.9 6.1 copy-start.9
  20.7 9.4 %collective-permute-start = (f32[2,8,512,128]{2,3,1,0:T(8,128)}, f32[2,8,512,128]{2,3,1,0:T(8,128)}, u32[]{:S(2)}, u32[]{:S(2)}) collective-permute-start(f32[2,8,512,128]{2,3,1,0:T(8,128)} %slice.757), channel_id=1, source_target_pairs={{8,0},{16,8},{24,16},{9,1},{17,9},{25,17},{10,2},{18,10},{26,18},{... | collective-permute-start | bytes 12582920 | tf_op jit(solution)/shard_map/ppermute | solution.py:14
  22.6 13.7 %copy-start.8 = (f32[2,32896]{1,0:T(2,128)}, f32[2,32896]{1,0:T(2,128)S(1)}, u32[]{:S(2)}) copy-start(f32[2,32896]{1,0:T(2,128)S(1)} %tile.10) | copy-start | bytes 789508
  52.1 8.8 %slice-start = ((f32[2,32896]{1,0:T(2,128)}), f32[2,32768]{1,0:T(2,128)S(1)}, s32[]{:S(2)}) async-start(f32[2,32896]{1,0:T(2,128)} %copy-done.8), calls=%async_computation.4 | async-start | bytes 524288 | tf_op jit(solution)/shard_map/slice | solution.py:27
  319.1 3.5 copy-start
  319.1 9.9 %copy-start.10 = (s32[64,2]{0,1:T(2,128)S(1)}, s32[64,2]{0,1:T(2,128)}, u32[]{:S(2)}) copy-start(s32[64,2]{0,1:T(2,128)} %param.21) | copy-start | bytes 1540
  322.6 3.3 copy-start.1
  325.9 11.0 %collective-permute-start.1 = (f32[2,1,64,256]{3,2,0,1:T(8,128)S(1)}, f32[2,1,64,256]{3,2,0,1:T(8,128)S(1)}, u32[]{:S(2)}, u32[]{:S(2)}) collective-permute-start(f32[2,1,64,256]{3,2,0,1:T(8,128)S(1)} %slice.769), channel_id=1, source_target_pairs={{1,0},{2,1},{3,2},{4,3},{5,4},{6,5},{7,6},{0,7},{9,8},{10,9},{11,1... | collective-permute-start | bytes 393224 | tf_op jit(solution)/shard_map/ppermute | solution.py:20
  480.1 4.5 copy-start.2
  503.7 1.2 copy-start.3
  516.1 3.5 copy-start.4
  548.4 11.4 %copy-start.5 = (f32[16,2,128,128]{3,0,1,2:T(8,128)S(1)}, f32[16,2,128,128]{3,0,1,2:T(8,128)}, u32[]{:S(2)}) copy-start(f32[16,2,128,128]{3,0,1,2:T(8,128)} %constant_dynamic-update-slice_fusion.3) | copy-start | bytes 6291460
  561.4 0.8 copy-start.6
  562.2 14.9 %copy-start.7 = (f32[16,2,32,128]{3,2,0,1:T(8,128)S(1)}, f32[16,2,32,128]{3,2,0,1:T(8,128)}, u32[]{:S(2)}) copy-start(f32[16,2,32,128]{3,2,0,1:T(8,128)} %copy-done.6) | copy-start | bytes 1572868
  593.9 98.8 %all-to-all-start.1 = ((f32[4,16,2,128,128]{4,3,2,1,0:T(8,128)}), f32[4,16,2,128,128]{4,3,2,1,0:T(8,128)}, u32[]{:S(2)}, u32[]{:S(2)}) async-start(f32[4,16,2,128,128]{4,3,2,1,0:T(8,128)} %stack.249), calls=%async_computation.1 | async-start | bytes 16777216 | tf_op jit(solution)/shard_map/all_to_all | solution.py:157
Sparse Core Ops, SparseCore 0:
  383.8 81.9 reduce-scatter.4
